TPU v7x, 256 devices: a whole 4x4x8 slice. The times are simulated.
256 devices in a mesh: row: 8 (over y, x_lo), col: 32 (over x_hi, z, core).
Axes of the slice: x: 4 (x_hi: 2, x_lo: 2; x = x_hi * 2 + x_lo), y: 4, z: 8, core: 2. Of those that a mesh axis runs over, the one named last changes fastest.
Arguments:
- density: float32 [4096, 4096], P('row', 'col'), as said below
- pattern: int32 [32, 6], replicated, may hold values from 0 to 31, as said below
Outputs:
- purified: float32 [4096, 4096], P('row', 'col')
Inputs may be any that keep to these rules, and one draw needn't show every extreme that they name: density is symmetric. `pattern`: each row lists 6 different block columns; the first is the row's own index.
All inputs are finite; a program needn't handle non-finite values.
Results may differ from a plain program's by a relative error of at most 0.00021.
Values sent between devices are 32-bit elements; how exact they have to be, the bound alone decides.
No kernel may reach another device: no remote copies, remote signals or barrier semaphores. Data moves between devices by JAX's collectives and lax.ppermute only.
A program may use at most 64 MiB of HBM per device.

v0:
```python
import jax
import jax.numpy as jnp
from jax import lax
from jax.sharding import PartitionSpec as P

BLK = 128
NNZ = 6
ITERS = 2


def product(left, right):
    return jnp.dot(left, right, precision=lax.Precision.HIGH, preferred_element_type=jnp.float32)


def gather_rows(tile, name):
    parts = lax.axis_size(name)
    copies = jnp.broadcast_to(tile[None], (parts,) + tile.shape)
    got = lax.all_to_all(copies, name, 0, 0)
    return got.reshape(parts * tile.shape[0], tile.shape[1])


def local(density, pattern):
    rows_dev, cols_dev = density.shape
    row_number = lax.axis_index("row")
    col_index = lax.axis_index("col")
    matrix_order = cols_dev * lax.axis_size("col")
    block_count = matrix_order // BLK
    tile_blocks = cols_dev // BLK
    row_blocks = rows_dev // BLK
    listed = jnp.any(
        pattern[:, :, None] == jnp.arange(block_count, dtype=jnp.int32)[None, None, :], axis=1
    ).astype(jnp.float32)
    block_live = jnp.maximum(listed, listed.T)
    my_rows = lax.dynamic_slice_in_dim(block_live, row_number * row_blocks, row_blocks, 0)
    own_blocks = lax.dynamic_slice_in_dim(my_rows, col_index * tile_blocks, tile_blocks, 1)
    pattern_mask = jnp.repeat(jnp.repeat(own_blocks, BLK, axis=0), BLK, axis=1)
    global_rows = row_number * rows_dev + jnp.arange(rows_dev, dtype=jnp.int32)
    global_cols = col_index * cols_dev + jnp.arange(cols_dev, dtype=jnp.int32)
    identity = (global_rows[:, None] == global_cols[None, :]).astype(jnp.float32)
    current = 0.5 * identity + 0.45 / jnp.sqrt(jnp.float32(2 * NNZ * BLK)) * pattern_mask * density
    for purify_round in range(ITERS):
        row_panel = lax.all_gather(current, "col", axis=1, tiled=True)
        column_panel = gather_rows(current, "row")
        square = pattern_mask * product(row_panel, column_panel)
        square_panel = gather_rows(square, "row")
        cube = pattern_mask * product(row_panel, square_panel)
        current = 3.0 * square - 2.0 * cube
    return current


def solution(mesh):
    return jax.shard_map(
        local,
        mesh=mesh,
        in_specs=(P("row", "col"), P()),
        out_specs=P("row", "col"),
        check_vma=False,
    )
```

profile of v0, /device:TPU:1, one launch (start us, length us, event | category | flops | bytes accessed | tf_op | source)
XLA Modules:
  0.0 322.7 jit_solution(1169803695684405316)
XLA Ops:
  6.5 0.0 all-gather.3.cloned.1.call-start
  6.5 0.8 fusion.4
  7.4 0.1 dynamic_slice.8
  7.4 0.1 copy.6
  7.5 0.1 fusion.5
  7.6 0.1 bitcast_multiply_fusion
  7.7 1.9 multiply_add_fusion
  9.5 0.0 all-gather.3.cloned.1.call-update
  9.6 2.5 broadcast_in_dim.14
  12.0 5.9 %all-to-all-start = ((f32[8,512,128]{2,1,0:T(8,128)}), f32[8,512,128]{2,1,0:T(8,128)S(1)}, u32[]{:S(2)}, u32[]{:S(2)}) async-start(f32[8,512,128]{2,1,0:T(8,128)} %broadcast_in_dim.14), calls=%async_computation | async-start | bytes 4194304 | tf_op jit(solution)/shard_map/all_to_all | solution.py:18
  18.0 0.0 all-gather.5.cloned.1.call-start
  18.0 0.1 broadcast_bitcast_fusion
  18.1 28.8 %all-to-all-done = f32[8,512,128]{2,1,0:T(8,128)S(1)} async-done(((f32[8,512,128]{2,1,0:T(8,128)}), f32[8,512,128]{2,1,0:T(8,128)S(1)}, u32[]{:S(2)}, u32[]{:S(2)}) %all-to-all-start) | async-done | bytes 2097184 | tf_op jit(solution)/shard_map/all_to_all | solution.py:18
  46.8 78.6 %all-gather.3.cloned.1.call-done = f32[512,4096]{1,0:T(8,128)} async-done(((f32[512,128]{1,0:T(8,128)}), f32[512,4096]{1,0:T(8,128)}) %all-gather.3.cloned.1.call-update) | async-done | bytes 8388624 | tf_op jit(solution)/shard_map/all_gather | solution.py:42
  125.5 0.0 copy-start
  125.5 6.7 %convolution_multiply_fusion.3 = f32[512,128]{1,0:T(8,128)S(1)} fusion(f32[512,4096]{1,0:T(8,128)} %all-gather.3.cloned.1.call-done, f32[4096,128]{1,0:T(8,128)S(1)} %bitcast.19, f32[512]{0:T(512)S(1)} %broadcast_bitcast_fusion), kind=kOutput, calls=%fused_computation.5 | convolution fusion | flops 1610678272 | bytes 10749952 | tf_op jit(solution)/shard_map/dot_general | solution.py:12
  132.2 0.1 broadcast_in_dim.15
  132.3 30.0 %all_to_all.20 = f32[8,512,128]{2,1,0:T(8,128)S(1)} all-to-all(f32[8,512,128]{2,1,0:T(8,128)S(1)} %broadcast_in_dim.15), channel_id=1, replica_groups=mesh['row'=8,'col'=32] {'row'}, dimensions={0} | all-to-all | bytes 4194304 | tf_op jit(solution)/shard_map/all_to_all | solution.py:18
  162.4 0.0 copy-done
  162.4 4.2 %fusion.2 = f32[512,128]{1,0:T(8,128)} fusion(f32[512,4096]{1,0:T(8,128)S(1)} %copy-done, f32[4096,128]{1,0:T(8,128)S(1)} %bitcast.22, f32[512,128]{1,0:T(8,128)S(1)} %convolution_multiply_fusion.3, f32[512]{0:T(512)S(1)} %broadcast_bitcast_fusion), kind=kOutput, calls=%fused_computation.6 | convolution fusion | flops 1610874880 | bytes 11012096 | tf_op jit(solution)/shard_map/dot_general | solution.py:12
  166.5 0.0 all-gather.5.cloned.1.call-update
  166.6 1.1 broadcast_in_dim.16
  167.7 32.1 %all_to_all.21 = f32[8,512,128]{2,1,0:T(8,128)S(1)} all-to-all(f32[8,512,128]{2,1,0:T(8,128)S(1)} %broadcast_in_dim.16), channel_id=1, replica_groups=mesh['row'=8,'col'=32] {'row'}, dimensions={0} | all-to-all | bytes 4194304 | tf_op jit(solution)/shard_map/all_to_all | solution.py:18
  199.8 75.0 %all-gather.5.cloned.1.call-done = f32[512,4096]{1,0:T(8,128)} async-done(((f32[512,128]{1,0:T(8,128)}), f32[512,4096]{1,0:T(8,128)}) %all-gather.5.cloned.1.call-update) | async-done | bytes 8388624 | tf_op jit(solution)/shard_map/all_gather | solution.py:42
  274.8 0.0 copy-start.1
  274.8 6.7 %convolution_multiply_fusion.1 = f32[512,128]{1,0:T(8,128)S(1)} fusion(f32[512,4096]{1,0:T(8,128)} %all-gather.5.cloned.1.call-done, f32[4096,128]{1,0:T(8,128)S(1)} %bitcast.20, f32[512]{0:T(512)S(1)} %broadcast_bitcast_fusion), kind=kOutput, calls=%fused_computation.2 | convolution fusion | flops 1610678272 | bytes 10749952 | tf_op jit(solution)/shard_map/dot_general | solution.py:12
  281.5 0.1 broadcast_in_dim.17
  281.7 30.0 %all_to_all.22 = f32[8,512,128]{2,1,0:T(8,128)S(1)} all-to-all(f32[8,512,128]{2,1,0:T(8,128)S(1)} %broadcast_in_dim.17), channel_id=1, replica_groups=mesh['row'=8,'col'=32] {'row'}, dimensions={0} | all-to-all | bytes 4194304 | tf_op jit(solution)/shard_map/all_to_all | solution.py:18
  311.7 0.0 copy-done.1
  311.7 4.2 %fusion.3 = f32[512,128]{1,0:T(8,128)} fusion(f32[512,4096]{1,0:T(8,128)S(1)} %copy-done.1, f32[4096,128]{1,0:T(8,128)S(1)} %bitcast.21, f32[512,128]{1,0:T(8,128)S(1)} %convolution_multiply_fusion.1, f32[512]{0:T(512)S(1)} %broadcast_bitcast_fusion), kind=kOutput, calls=%fused_computation.7 | convolution fusion | flops 1610874880 | bytes 11012096 | tf_op jit(solution)/shard_map/dot_general | solution.py:12
  (3 shorter events, 0.0 us)
Async XLA Ops:
  6.5 118.9 %all-gather.3.cloned.1.call-start = ((), (), s32[]{:S(2)}) async-start(), calls=%async_computation.4 | async-start | bytes 8650752 | tf_op jit(solution)/shard_map/all_gather | solution.py:42
  12.0 34.8 %all-to-all-start = ((f32[8,512,128]{2,1,0:T(8,128)}), f32[8,512,128]{2,1,0:T(8,128)S(1)}, u32[]{:S(2)}, u32[]{:S(2)}) async-start(f32[8,512,128]{2,1,0:T(8,128)} %broadcast_in_dim.14), calls=%async_computation | async-start | bytes 4194304 | tf_op jit(solution)/shard_map/all_to_all | solution.py:18
  18.0 256.8 %all-gather.5.cloned.1.call-start = ((), (), s32[]{:S(2)}) async-start(), calls=%async_computation.5 | async-start | bytes 8650752 | tf_op jit(solution)/shard_map/all_gather | solution.py:42
  125.5 36.9 %copy-start = (f32[512,4096]{1,0:T(8,128)S(1)}, f32[512,4096]{1,0:T(8,128)}, u32[]{:S(2)}) copy-start(f32[512,4096]{1,0:T(8,128)} %all-gather.3.cloned.1.call-done) | copy-start | bytes 25165828
  274.8 36.9 %copy-start.1 = (f32[512,4096]{1,0:T(8,128)S(1)}, f32[512,4096]{1,0:T(8,128)}, u32[]{:S(2)}) copy-start(f32[512,4096]{1,0:T(8,128)} %all-gather.5.cloned.1.call-done) | copy-start | bytes 25165828
Sparse Core Ops, SparseCore 0:
  9.9 115.5 all-gather.2
  166.7 108.0 all-gather.4
where the time goes:
time: 323 us
  waiting for transfers between devices  182 us (56%)
  blocking collectives  92.2 us (29%)
  matrix products  21.7 us (7%)
  between operations  13.5 us (4%)
  starting transfers between devices  5.99 us (2%)
  local copies, waits for them, and re-layouts  4.07 us (1%)
    all_gather x2, waiting for transfers between devices, local(): row_panel = lax.all_gather(current, 'col', axis=1, tiled=True)  154 us
    all_to_all x3, blocking collectives, gather_rows(): got = lax.all_to_all(copies, name, 0, 0)  92.2 us
    all_to_all x1, waiting for transfers between devices, gather_rows(): got = lax.all_to_all(copies, name, 0, 0)  28.8 us
    dot_general x4, matrix products, product(): jnp.dot(left, right, precision=lax.Precision.HIGH, preferred_element_type...  21.7 us
  transfers between devices with their start and end apart: 3, of which 3 were waited for; matrix products, arithmetic and copies ran while one was open for 1% of the time, Pallas kernels for 0%

commit v1 on v0

--- a/solution.py
+++ b/solution.py
@@ -6,6 +6,11 @@
 BLK = 128
 NNZ = 6
 ITERS = 2
+
+
+def swapped_in(x, axis, dim):
+    sent = jnp.stack([x] * lax.axis_size(axis))
+    return jnp.concatenate(lax.all_to_all(sent, axis, 0, 0), axis=dim)
 
 
 def product(left, right):
@@ -39,7 +44,7 @@
     identity = (global_rows[:, None] == global_cols[None, :]).astype(jnp.float32)
     current = 0.5 * identity + 0.45 / jnp.sqrt(jnp.float32(2 * NNZ * BLK)) * pattern_mask * density
     for purify_round in range(ITERS):
-        row_panel = lax.all_gather(current, "col", axis=1, tiled=True)
+        row_panel = swapped_in(current, "col", 1)
         column_panel = gather_rows(current, "row")
         square = pattern_mask * product(row_panel, column_panel)
         square_panel = gather_rows(square, "row")

time: 323 us -> 559 us (1.73)
  blocking collectives: 92.2 us -> 255 us
  waiting for transfers between devices: 182 us -> 235 us
  starting transfers between devices: 5.99 us -> 22.3 us
  between operations: 13.5 us -> 0.12 us
  matrix products: 21.7 us -> 32.5 us
    all_to_all x0 -> x1, blocking collectives: none -> 200 us  [swapped_in(): return jnp.concatenate(lax.all_to_all(sent, axis, 0, 0), axis=dim)]
    all_to_all x0 -> x1, waiting for transfers between devices: none -> 186 us  [swapped_in(): return jnp.concatenate(lax.all_to_all(sent, axis, 0, 0), axis=dim)]
    all_gather x2 -> x0, waiting for transfers between devices: 154 us -> none  [local(): row_panel = lax.all_gather(current, 'col', axis=1, tiled=True)]
    all_to_all x3 -> x2, blocking collectives: 92.2 us -> 54.5 us  [gather_rows(): got = lax.all_to_all(copies, name, 0, 0)]
    all_to_all x1 -> x2, waiting for transfers between devices: 28.8 us -> 49.4 us  [gather_rows(): got = lax.all_to_all(copies, name, 0, 0)]
    all_to_all x0 -> x1, starting transfers between devices: none -> 12.7 us  [swapped_in(): return jnp.concatenate(lax.all_to_all(sent, axis, 0, 0), axis=dim)]
    dot_general x4, matrix products: 21.7 us -> 32.5 us  [product(): jnp.dot(left, right, precision=lax.Precision.HIGH, preferred_element_type...]
  transfers between devices with their start and end apart: 3 -> 3, of which waited for: 3 -> 3; matrix products, arithmetic and copies ran while one was open for 1% -> 0% of each run, Pallas kernels for 0% -> 0%
where the time goes in v1:
time: 559 us; the launch traced here: 556 us
  blocking collectives  255 us (46%)
  waiting for transfers between devices  235 us (42%)
  matrix products  32.5 us (6%)
  starting transfers between devices  22.3 us (4%)
  local copies, waits for them, and re-layouts  9.05 us (2%)
    all_to_all x1, blocking collectives, swapped_in(): return jnp.concatenate(lax.all_to_all(sent, axis, 0, 0), axis=dim)  200 us
    all_to_all x1, waiting for transfers between devices, swapped_in(): return jnp.concatenate(lax.all_to_all(sent, axis, 0, 0), axis=dim)  186 us
    all_to_all x2, blocking collectives, gather_rows(): got = lax.all_to_all(copies, name, 0, 0)  54.5 us
    all_to_all x2, waiting for transfers between devices, gather_rows(): got = lax.all_to_all(copies, name, 0, 0)  49.4 us
    dot_general x4, matrix products, product(): jnp.dot(left, right, precision=lax.Precision.HIGH, preferred_element_type...  32.5 us
    all_to_all x1, starting transfers between devices, swapped_in(): return jnp.concatenate(lax.all_to_all(sent, axis, 0, 0), axis=dim)  12.7 us
  transfers between devices with their start and end apart: 3, of which 3 were waited for; matrix products, arithmetic and copies ran while one was open for 0% of the time, Pallas kernels for 0%

profile of v1, /device:TPU:1, one launch (start us, length us, event | category | flops | bytes accessed | tf_op | source)
XLA Modules:
  0.0 555.5 jit_solution(10062860997380130297)
XLA Ops:
  0.0 0.8 fusion.4
  0.8 0.1 dynamic_slice.8
  0.9 0.1 copy.12
  1.0 0.1 fusion.5
  1.1 0.1 bitcast_multiply_fusion
  1.1 1.1 multiply_add_fusion
  2.3 1.5 broadcast_in_dim.14
  3.8 5.9 %all-to-all-start.1 = ((f32[8,512,128]{2,1,0:T(8,128)}), f32[8,512,128]{2,1,0:T(8,128)S(1)}, u32[]{:S(2)}, u32[]{:S(2)}) async-start(f32[8,512,128]{2,1,0:T(8,128)} %broadcast_in_dim.14), calls=%async_computation.1 | async-start | bytes 4194304 | tf_op jit(solution)/shard_map/all_to_all | solution.py:23
  9.7 0.1 copy.10
  9.8 25.9 %all-to-all-done.1 = f32[8,512,128]{2,1,0:T(8,128)S(1)} async-done(((f32[8,512,128]{2,1,0:T(8,128)}), f32[8,512,128]{2,1,0:T(8,128)S(1)}, u32[]{:S(2)}, u32[]{:S(2)}) %all-to-all-start.1) | async-done | bytes 2097184 | tf_op jit(solution)/shard_map/all_to_all | solution.py:23
  35.8 4.3 stack.4
  40.1 12.7 %all-to-all-start = ((f32[32,512,128]{1,2,0:T(8,128)}), f32[32,512,128]{1,2,0:T(8,128)}, u32[]{:S(2)}, u32[]{:S(2)}) async-start(f32[32,512,128]{1,2,0:T(8,128)} %stack.4), calls=%async_computation | async-start | bytes 16777216 | tf_op jit(solution)/shard_map/all_to_all | solution.py:13
  52.8 0.1 broadcast_bitcast_fusion
  52.9 185.5 %all-to-all-done = f32[32,512,128]{1,2,0:T(8,128)} async-done(((f32[32,512,128]{1,2,0:T(8,128)}), f32[32,512,128]{1,2,0:T(8,128)}, u32[]{:S(2)}, u32[]{:S(2)}) %all-to-all-start) | async-done | bytes 8388640 | tf_op jit(solution)/shard_map/all_to_all | solution.py:13
  238.4 9.1 %convolution_multiply_fusion.3 = f32[512,128]{1,0:T(8,128)S(1)} fusion(f32[512,4096]{0,1:T(8,128)} %bitcast.4, f32[4096,128]{1,0:T(8,128)S(1)} %bitcast.27, f32[512]{0:T(512)S(1)} %broadcast_bitcast_fusion), kind=kOutput, calls=%fused_computation.5 | convolution fusion | flops 1610678272 | bytes 10749952 | tf_op jit(solution)/shard_map/dot_general | solution.py:17
  247.4 0.1 broadcast_in_dim.15
  247.6 27.2 %all_to_all.30 = f32[8,512,128]{2,1,0:T(8,128)S(1)} all-to-all(f32[8,512,128]{2,1,0:T(8,128)S(1)} %broadcast_in_dim.15), channel_id=1, replica_groups=mesh['row'=8,'col'=32] {'row'}, dimensions={0} | all-to-all | bytes 4194304 | tf_op jit(solution)/shard_map/all_to_all | solution.py:23
  274.8 9.1 %fusion.2 = f32[512,128]{1,0:T(8,128)S(1)} fusion(f32[512,4096]{0,1:T(8,128)} %bitcast.4, f32[4096,128]{1,0:T(8,128)S(1)} %bitcast.30, f32[512,128]{1,0:T(8,128)S(1)} %convolution_multiply_fusion.3, f32[512]{0:T(512)S(1)} %broadcast_bitcast_fusion), kind=kOutput, calls=%fused_computation.6 | convolution fusion | flops 1610874880 | bytes 11012096 | tf_op jit(solution)/shard_map/dot_general | solution.py:17
  283.9 1.5 broadcast_in_dim.16
  285.4 3.6 all-to-all-start.4
  289.0 0.1 copy.11
  289.2 23.5 %all-to-all-done.4 = f32[8,512,128]{2,1,0:T(8,128)S(1)} async-done(((f32[8,512,128]{2,1,0:T(8,128)}), f32[8,512,128]{2,1,0:T(8,128)S(1)}, u32[]{:S(2)}, u32[]{:S(2)}) %all-to-all-start.4) | async-done | bytes 2097184 | tf_op jit(solution)/shard_map/all_to_all | solution.py:23
  312.6 1.1 stack.5
  313.7 200.0 %all_to_all.31 = f32[32,512,128]{1,2,0:T(8,128)S(1)} all-to-all(f32[32,512,128]{1,2,0:T(8,128)S(1)} %stack.5), channel_id=1, replica_groups=mesh['row'=8,'col'=32] {'col'}, dimensions={0} | all-to-all | bytes 16777216 | tf_op jit(solution)/shard_map/all_to_all | solution.py:13
  513.7 6.9 %convolution_multiply_fusion.1 = f32[512,128]{1,0:T(8,128)S(1)} fusion(f32[512,4096]{0,1:T(8,128)S(1)} %bitcast.25, f32[4096,128]{1,0:T(8,128)S(1)} %bitcast.28, f32[512]{0:T(512)S(1)} %broadcast_bitcast_fusion), kind=kOutput, calls=%fused_computation.2 | convolution fusion | flops 1610678272 | bytes 10749952 | tf_op jit(solution)/shard_map/dot_general | solution.py:17
  520.6 0.1 broadcast_in_dim.17
  520.7 27.3 %all_to_all.32 = f32[8,512,128]{2,1,0:T(8,128)S(1)} all-to-all(f32[8,512,128]{2,1,0:T(8,128)S(1)} %broadcast_in_dim.17), channel_id=1, replica_groups=mesh['row'=8,'col'=32] {'row'}, dimensions={0} | all-to-all | bytes 4194304 | tf_op jit(solution)/shard_map/all_to_all | solution.py:23
  548.1 7.5 %fusion.3 = f32[512,128]{1,0:T(8,128)} fusion(f32[512,4096]{0,1:T(8,128)S(1)} %bitcast.26, f32[4096,128]{1,0:T(8,128)S(1)} %bitcast.29, f32[512,128]{1,0:T(8,128)S(1)} %convolution_multiply_fusion.1, f32[512]{0:T(512)S(1)} %broadcast_bitcast_fusion), kind=kOutput, calls=%fused_computation.7 | convolution fusion | flops 1610874880 | bytes 11012096 | tf_op jit(solution)/shard_map/dot_general | solution.py:17
  (3 shorter events, 0.0 us)
Async XLA Ops:
  3.8 32.0 %all-to-all-start.1 = ((f32[8,512,128]{2,1,0:T(8,128)}), f32[8,512,128]{2,1,0:T(8,128)S(1)}, u32[]{:S(2)}, u32[]{:S(2)}) async-start(f32[8,512,128]{2,1,0:T(8,128)} %broadcast_in_dim.14), calls=%async_computation.1 | async-start | bytes 4194304 | tf_op jit(solution)/shard_map/all_to_all | solution.py:23
  40.1 198.3 %all-to-all-start = ((f32[32,512,128]{1,2,0:T(8,128)}), f32[32,512,128]{1,2,0:T(8,128)}, u32[]{:S(2)}, u32[]{:S(2)}) async-start(f32[32,512,128]{1,2,0:T(8,128)} %stack.4), calls=%async_computation | async-start | bytes 16777216 | tf_op jit(solution)/shard_map/all_to_all | solution.py:13
  285.4 27.2 %all-to-all-start.4 = ((f32[8,512,128]{2,1,0:T(8,128)}), f32[8,512,128]{2,1,0:T(8,128)S(1)}, u32[]{:S(2)}, u32[]{:S(2)}) async-start(f32[8,512,128]{2,1,0:T(8,128)} %broadcast_in_dim.16), calls=%async_computation.4 | async-start | bytes 4194304 | tf_op jit(solution)/shard_map/all_to_all | solution.py:23
